TPU v7x, 32 devices: a whole 2x2x4 slice. The times are simulated.
32 devices in a mesh: seq: 8 (over y, x, core), head: 4 (over z).
Axes of the slice: x: 2, y: 2, z: 4, core: 2. Of those that a mesh axis runs over, the one named last changes fastest.
Arguments:
- queries: bfloat16 [2048, 16, 128], P('seq', 'head'), may hold values from -30 to 30
- keys: bfloat16 [2048, 16, 128], P('seq', 'head'), may hold values from -12 to 12
- values: bfloat16 [2048, 16, 128], P('seq', 'head'), may hold values from -6 to 6
- log_forget: float32 [16, 2048], P('head', 'seq'), may hold values from -1.6 to 0
- strength: float32 [16, 2048], P('head', 'seq'), may hold values from 0.05 to 1
- out_weight: bfloat16 [2048, 2048], P('head'), may hold values from -0.125 to 0.125
Outputs:
- mixed: bfloat16 [2048, 2048], P(('seq', 'head'))
All inputs are finite; a program needn't handle non-finite values.
Results may differ from a plain program's by a relative error of at most 0.018.
Values may be sent and summed in bfloat16 or wider, within the bound.
A program may use at most 64 MiB of HBM per device.

v0:
```python
import jax
import jax.numpy as jnp
from jax import lax
from jax.sharding import PartitionSpec as P

WINDOW = 1024
CG_STEPS = 6


ridge = 0.25
highest = lax.Precision.HIGHEST
tiny_floor = 1e-30


def shifted(x, axis, by):
    devices = lax.axis_size(axis)
    pairs = [(i, i + by) for i in range(devices) if 0 <= i + by < devices]
    return lax.ppermute(x, axis, pairs)


def carried_in(x, axis, combine, identity):
    devices, mine = (lax.axis_size(axis), lax.axis_index(axis))
    everything = jax.tree.map(
        lambda part, kind: lax.all_gather(part.astype(kind), axis),
        x,
        (jnp.bfloat16, jnp.bfloat16, jnp.bfloat16),
    )
    start = jax.tree.map(
        lambda part, zero: jnp.broadcast_to(jnp.asarray(zero, part.dtype), part.shape), x, identity
    )

    def hop(k, before):
        reached = k < mine
        new = combine(
            before, jax.tree.map(lambda part, own: part[k].astype(own.dtype), everything, x)
        )
        return jax.tree.map(lambda a, b: jnp.where(reached, a, b), new, before)

    return lax.fori_loop(0, devices, hop, start)


def window_attention(query_rows, key_rows, value_rows, offset):
    count = query_rows.shape[0]
    block = min(512, count)
    reach = WINDOW + block
    scale = query_rows.shape[2] ** (-0.5)
    query_pos = 0 + jnp.arange(block)
    key_pos = 0 - WINDOW + jnp.arange(reach)
    admitted = (
        (key_pos[None, :] <= query_pos[:, None])
        & (key_pos[None, :] > query_pos[:, None] - WINDOW)
        & (key_pos[None, :] + offset >= 0)
    )
    scores = (
        jnp.einsum("qhe,khe->hqk", query_rows, key_rows, preferred_element_type=jnp.float32) * scale
    )
    scores = jnp.where(admitted[None], scores, -jnp.inf)
    largest = jnp.max(scores, axis=-1, keepdims=True)
    expo = jnp.exp(scores - largest)
    weights = (expo / jnp.sum(expo, axis=-1, keepdims=True)).astype(jnp.bfloat16)
    results = jnp.einsum("hqk,khe->qhe", weights, value_rows, preferred_element_type=jnp.float32)
    return results


def group_step(state, inputs):
    key_state, value_state = state
    query_part, key_part, value_part, forget_part, strength_part = inputs
    decay_sum = jnp.cumsum(forget_part, axis=1)
    length = forget_part.shape[1]
    order = jnp.arange(length)
    causal = (order[:, None] >= order[None, :])[None]
    gap = jnp.where(causal, decay_sum[:, :, None] - decay_sum[:, None, :], 0.0)
    mixing = jnp.where(causal, jnp.exp(gap), 0.0) * strength_part[:, None, :]
    leading = jnp.exp(decay_sum)[:, :, None]
    solution = jnp.zeros_like(query_part)
    residual = query_part
    direction = query_part
    norm_now = jnp.sum(residual * residual, axis=-1, keepdims=True)
    for iteration in range(CG_STEPS):
        operator_correlation = jnp.einsum("htf,hsf->hts", direction, key_part, precision=highest)
        carried = jnp.einsum("htf,hef->hte", direction, key_state, precision=highest)
        inside = jnp.einsum(
            "hts,hse->hte", mixing * operator_correlation, key_part, precision=highest
        )
        image = leading * carried + inside + ridge * direction
        alpha = norm_now / jnp.maximum(
            jnp.sum(direction * image, axis=-1, keepdims=True), tiny_floor
        )
        solution = solution + alpha * direction
        residual = residual - alpha * image
        norm_next = jnp.sum(residual * residual, axis=-1, keepdims=True)
        direction = residual + norm_next / jnp.maximum(norm_now, tiny_floor) * direction
        norm_now = norm_next
    correlation = jnp.einsum("htf,hsf->hts", solution, key_part, precision=highest)
    output = leading * jnp.einsum("htf,hef->hte", solution, value_state, precision=highest)
    output = output + jnp.einsum(
        "hts,hse->hte", mixing * correlation, value_part, precision=highest
    )
    tail = jnp.exp(decay_sum[:, -1:] - decay_sum) * strength_part
    end_factor = jnp.exp(decay_sum[:, -1])[:, None, None]
    key_state = end_factor * key_state + jnp.einsum(
        "hse,hsf->hef", tail[:, :, None] * key_part, key_part, precision=highest
    )
    value_state = end_factor * value_state + jnp.einsum(
        "hse,hsf->hef", tail[:, :, None] * value_part, key_part, precision=highest
    )
    return ((key_state, value_state), output)


def normalized(rows):
    wide = rows.astype(jnp.float32)
    return wide * lax.rsqrt(jnp.sum(wide * wide, axis=-1, keepdims=True) + 1e-06)


def mesa_heads(query_rows, key_rows, value_rows, log_forget, strength, key_start, value_start):
    heads_here, count, width = query_rows.shape
    group = min(256, count)
    blocks = count // group

    def blocked(array):
        shaped = array.reshape((heads_here, blocks, group) + array.shape[2:])
        return jnp.moveaxis(shaped, 1, 0)

    inputs = (
        blocked(query_rows),
        blocked(key_rows),
        blocked(value_rows),
        blocked(log_forget),
        blocked(strength),
    )
    final, outputs = lax.scan(group_step, (key_start, value_start), inputs)
    return jnp.moveaxis(outputs, 0, 1).reshape(heads_here, count, width)


def join_states(earlier, later):
    factor = jnp.exp(later[0])[:, None, None]
    return (earlier[0] + later[0], factor * earlier[1] + later[1], factor * earlier[2] + later[2])


def on_device(queries, keys, values, log_forget, strength, out_weight):
    tok_rows, heads_dev, width = queries.shape
    position = lax.axis_index("seq")
    halo_rows = min(tok_rows, WINDOW)
    distance_count = WINDOW // halo_rows
    stacked = jnp.stack((keys, values))
    earlier_parts = []
    for distance in range(distance_count, 0, -1):
        earlier_parts.append(shifted(stacked, "seq", distance))
    earlier_rows = jnp.concatenate(earlier_parts, axis=1)
    key_window = jnp.concatenate((earlier_rows[0], keys), axis=0)
    value_window = jnp.concatenate((earlier_rows[1], values), axis=0)
    attended = window_attention(queries, key_window, value_window, position * tok_rows)
    query_norm = jnp.transpose(normalized(queries), (1, 0, 2))
    key_norm = jnp.transpose(normalized(keys), (1, 0, 2))
    value_wide = jnp.transpose(values.astype(jnp.float32), (1, 0, 2))
    decay_sum = jnp.cumsum(log_forget, axis=1)
    decay_total = decay_sum[:, -1]
    tail = jnp.exp(decay_total[:, None] - decay_sum) * strength
    key_local = jnp.einsum("hse,hsf->hef", tail[:, :, None] * key_norm, key_norm, precision=highest)
    value_local = jnp.einsum(
        "hse,hsf->hef", tail[:, :, None] * value_wide, key_norm, precision=highest
    )
    empty = jnp.zeros((heads_dev, width, width), jnp.float32)
    identity = (jnp.zeros((heads_dev,), jnp.float32), empty, empty)
    prefix_state = carried_in((decay_total, key_local, value_local), "seq", join_states, identity)
    key_start, value_start = (prefix_state[1], prefix_state[2])
    mesa = mesa_heads(
        query_norm, key_norm, value_wide, log_forget, strength, key_start, value_start
    )
    head_out = (attended + jnp.transpose(mesa, (1, 0, 2))).astype(jnp.bfloat16)
    flat_local = head_out.reshape(tok_rows, heads_dev * width)
    return lax.psum_scatter(
        jnp.dot(flat_local, out_weight, preferred_element_type=jnp.float32).astype(jnp.bfloat16),
        "head",
        scatter_dimension=0,
        tiled=True,
    )


def solution(mesh):
    in_specs = (
        P("seq", "head", None),
        P("seq", "head", None),
        P("seq", "head", None),
        P("head", "seq"),
        P("head", "seq"),
        P("head", None),
    )
    out_specs = P(("seq", "head"), None)
    return jax.shard_map(
        on_device, mesh=mesh, in_specs=in_specs, out_specs=out_specs, check_vma=False
    )
```

profile of v0, /device:TPU:4, one launch (start us, length us, event | category | flops | bytes accessed | tf_op | source)
XLA Modules:
  0.0 165.5 jit_solution(12567280476320945277)
XLA Ops:
  6.5 0.8 reshape.281
  7.4 1.2 reduce-window.12
  10.1 1.3 fusion.55
  11.5 1.3 fusion.56
  12.8 2.7 %convert_multiply_fusion.4 = (f32[4,256,128]{2,0,1:T(4,128)}, f32[4,256,128]{2,0,1:T(4,128)S(1)}) fusion(f32[4,256]{0,1:T(8,128)S(1)} %copy.121, bf16[256,4,128]{2,1,0:T(4,128)(2,1)} %param.10, f32[256,4]{1,0:T(8,128)S(1)} %add_rsqrt_fusion, bf16[256,4,128]{2,1,0:T(4,128)(2,1)} %param.9), kind=kLoop, calls=%fused_computation.105 | loop fusion | flops 655360 | bytes 1581056 | tf_op jit(solution)/shard_map/mul | solution.py:161
  15.5 1.7 %convolution_convert_fusion.2 = bf16[4,128,128]{2,1,0:T(8,128)(2,1)} fusion(f32[4,256,128]{2,0,1:T(4,128)S(1)} %get-tuple-element.214, f32[4,256,128]{2,0,1:T(4,128)S(1)} %fusion.56), kind=kOutput, calls=%fused_computation.59 | convolution fusion | flops 201392128 | bytes 1179648 | tf_op jit(solution)/shard_map/hse,hsf->hef/dot_general | solution.py:159
  17.3 1.0 copy_bitcast_fusion.2
  19.1 1.3 collective-permute-start
  20.4 2.8 %collective-permute-start.1 = (bf16[2,256,4,128]{3,1,2,0:T(8,128)(2,1)}, bf16[2,256,4,128]{3,1,2,0:T(8,128)(2,1)}, u32[]{:S(2)}, u32[]{:S(2)}) collective-permute-start(bf16[2,256,4,128]{3,1,2,0:T(8,128)(2,1)} %pad_maximum_fusion), channel_id=1, source_target_pairs={{0,12},{4,16},{8,20},{12,24},{16,28},{1,13},{5,17},{9,21},{13,25},... | collective-permute-start | bytes 1572872 | tf_op jit(solution)/shard_map/ppermute | solution.py:18
  23.2 1.9 %collective-permute-start.2 = (bf16[2,256,4,128]{3,1,2,0:T(8,128)(2,1)}, bf16[2,256,4,128]{3,1,2,0:T(8,128)(2,1)}, u32[]{:S(2)}, u32[]{:S(2)}) collective-permute-start(bf16[2,256,4,128]{3,1,2,0:T(8,128)(2,1)} %pad_maximum_fusion), channel_id=1, source_target_pairs={{0,8},{4,12},{8,16},{12,20},{16,24},{20,28},{1,9},{5,13},{9,17},{1... | collective-permute-start | bytes 1572872 | tf_op jit(solution)/shard_map/ppermute | solution.py:18
  25.2 1.9 %collective-permute-start.3 = (bf16[2,256,4,128]{3,1,2,0:T(8,128)(2,1)}, bf16[2,256,4,128]{3,1,2,0:T(8,128)(2,1)}, u32[]{:S(2)}, u32[]{:S(2)}) collective-permute-start(bf16[2,256,4,128]{3,1,2,0:T(8,128)(2,1)} %pad_maximum_fusion), channel_id=1, source_target_pairs={{0,4},{4,8},{8,12},{12,16},{16,20},{20,24},{24,28},{1,5},{5,9},{9,... | collective-permute-start | bytes 1572872 | tf_op jit(solution)/shard_map/ppermute | solution.py:18
  27.1 1.7 %convolution_convert_fusion.1 = bf16[4,128,128]{2,1,0:T(8,128)(2,1)} fusion(f32[4,256,128]{2,0,1:T(4,128)S(1)} %copy-done.6, f32[4,256,128]{2,0,1:T(4,128)S(1)} %fusion.56), kind=kOutput, calls=%fused_computation.58 | convolution fusion | flops 201392128 | bytes 1179648 | tf_op jit(solution)/shard_map/hse,hsf->hef/dot_general | solution.py:160
  29.2 1.6 fusion.15
  32.5 25.5 %all-reduce = bf16[32]{0:T(256)(128)(2,1)S(1)} all-reduce(bf16[32]{0:T(256)(128)(2,1)S(1)} %dynamic-update-slice), channel_id=2, replica_groups=mesh['seq'=8,'head'=4] {'seq'}, use_global_device_ids=true, to_apply=%add | all-reduce | flops 32 | bytes 128
  58.0 1.2 copy.131
  59.3 3.3 %convolution_multiply_fusion.6 = f32[4,256,256]{2,1,0:T(8,128)} fusion(bf16[256,4,128]{0,2,1:T(8,128)(2,1)S(1)} %copy.120, f32[4,256]{1,0:T(4,128)S(1)} %copy-done.10, f32[4,256]{1,0:T(4,128)S(1)} %bitcast.153, pred[256,256]{1,0:T(8,128)(4,1)S(1)} %iota_compare_fusion.1, f32[4,256,128]{2,0,1:T(4,128)} %copy-done.1, f32[256,4]{0,1:T(4,128)S(1)} %add_rsqrt_fusion.1), kind=kOutput, calls=%fused_computation.21 | convolution fusion | flops 404226048 | bytes 1912832 | tf_op jit(solution)/shard_map/while/body/eval_jaxpr/htf,hsf->hts/dot_general | solution.py:80
  62.6 1.1 constant_dynamic-update-slice_fusion.3
  63.7 3.7 %collective-permute-done.1 = bf16[2,256,4,128]{3,1,2,0:T(8,128)(2,1)} collective-permute-done((bf16[2,256,4,128]{3,1,2,0:T(8,128)(2,1)}, bf16[2,256,4,128]{3,1,2,0:T(8,128)(2,1)}, u32[]{:S(2)}, u32[]{:S(2)}) %collective-permute-start.1) | collective-permute-done | bytes 524320 | tf_op jit(solution)/shard_map/ppermute | solution.py:18
  67.4 1.1 constant_dynamic-update-slice_fusion.2
  68.6 1.1 constant_dynamic-update-slice_fusion.1
  69.7 1.1 constant_dynamic-update-slice_fusion
  70.8 1.5 slice_bitcast_fusion.1
  72.4 3.2 %exponential_reduce_fusion = f32[4,256]{1,0:T(4,128)S(1)} fusion(bf16[256,4,128]{0,2,1:T(8,128)(2,1)S(1)} %copy.120, pred[256,1280]{0,1:T(8,128)(4,1)} %fusion.15, bf16[256,4,128]{2,0,1:T(8,128)(2,1)} %get-tuple-element.212, bf16[1024,4,128]{2,0,1:T(8,128)(2,1)} %get-tuple-element.208), kind=kOutput, calls=%fused_computation.12 | convolution fusion | flops 343409920 | bytes 1904640 | tf_op jit(solution)/shard_map/sub | solution.py:59
  75.6 15.6 %all-gather.8.cloned.1.call-done = bf16[32,128,128]{2,1,0:T(8,128)(2,1)} async-done(((bf16[4,128,128]{2,1,0:T(8,128)(2,1)}), bf16[32,128,128]{2,1,0:T(8,128)(2,1)}) %all-gather.8.cloned.1.call-update) | async-done | bytes 1048592 | tf_op jit(solution)/shard_map/all_gather | solution.py:24
  91.1 9.4 %while.10 = (s32[]{:T(128)}, f32[4,128,128]{2,1,0:T(8,128)S(1)}, f32[4,128,128]{2,1,0:T(8,128)S(1)}, s32[]{:T(128)}, bf16[8,4]{1,0:T(8,128)(2,1)S(1)}, /*index=5...) while((s32[]{:T(128)}, f32[4,128,128]{2,1,0:T(8,128)S(1)}, ...), condition=%wide.region_8.9_spmd.clone, body=%wide.region_7.8_spmd.clone.sunk | while | flops 655368 | bytes 1310881 | solution.py:39
  91.1 1.1 fusion.134
  92.3 1.1 fusion.134
  93.4 1.1 fusion.134
  94.6 1.1 fusion.134
  95.7 1.1 fusion.134
  96.9 1.1 fusion.134
  98.0 1.1 fusion.134
  99.2 1.1 fusion.134
  101.1 2.6 %fusion.48 = (f32[4,256]{1,0:T(4,128)S(1)}, f32[4,256]{1,0:T(4,128)S(1)}, f32[4,256,128]{1,2,0:T(8,128)S(1)}) fusion(bf16[256,4,128]{0,2,1:T(8,128)(2,1)S(1)} %copy.120, f32[256,4]{0,1:T(4,128)S(1)} %add_rsqrt_fusion.1, f32[4,256,128]{1,2,0:T(8,128)S(1)} %convolution_multiply_fusion.12, f32[4,256,256]{2,1,0:T(8,128)} %convolution_multiply_fusion.6, ...), kind=kOutput, calls=%fused_computation.76 | convolution fusion | flops 403830784 | bytes 2895872 | tf_op jit(solution)/shard_map/while/body/eval_jaxpr/hts,hse->hte/dot_general | solution.py:82
  104.0 1.3 convolution_multiply_fusion.5
  105.9 1.3 multiply_reduce_fusion.7
  107.4 1.3 convolution_multiply_fusion.4
  109.4 1.3 multiply_reduce_fusion.5
  110.8 1.3 convolution_multiply_fusion.3
  112.8 1.3 multiply_reduce_fusion.3
  114.2 1.5 convolution_multiply_fusion.2
  116.4 1.3 multiply_reduce_fusion.1
  117.9 1.3 convolution_multiply_fusion.1
  119.8 1.3 fusion.34
  121.4 1.3 convolution_multiply_fusion
  124.1 4.8 %fusion.31 = bf16[256,4,128]{0,2,1:T(8,128)(2,1)} fusion(f32[256,4,128]{0,2,1:T(8,128)S(1)} %fusion.25, f32[4,256]{1,0:T(4,128)S(1)} %exponential_reduce_fusion, bf16[256,4,128]{2,0,1:T(8,128)(2,1)S(1)} %copy-done.9, bf16[1024,4,128]{2,0,1:T(8,128)(2,1)} %get-tuple-element.207, bf16[256,4,128]{0,2,1:T(8,128)(2,1)S(1)} %copy.120, ...), kind=kOutput, calls=%fused_computation.56 | convolution fusion | flops 683149568 | bytes 4001792 | tf_op jit(solution)/shard_map/hqk,khe->qhe/dot_general | solution.py:61
  128.9 2.7 %convolution_convert_fusion = bf16[256,2048]{1,0:T(8,128)(2,1)} fusion(bf16[256,512]{0,1:T(8,128)(2,1)} %bitcast.150, bf16[512,2048]{1,0:T(8,128)(2,1)S(1)} %copy-done), kind=kOutput, calls=%fused_computation.14 | convolution fusion | flops 537395200 | bytes 3407872 | tf_op jit(solution)/shard_map/dot_general | solution.py:173
  131.5 27.5 %reduce-scatter.2.cloned.1.call-done = bf16[64,2048]{1,0:T(8,128)(2,1)} async-done(((bf16[256,2048]{1,0:T(8,128)(2,1)}), bf16[64,2048]{1,0:T(8,128)(2,1)}) %reduce-scatter.2.cloned.1.call-update) | async-done | bytes 262160 | tf_op jit(solution)/shard_map/reduce_scatter | solution.py:172
  (98 shorter events, 10.4 us)
Async XLA Ops:
  6.5 122.3 %copy-start = (bf16[512,2048]{1,0:T(8,128)(2,1)S(1)}, bf16[512,2048]{1,0:T(8,128)(2,1)}, u32[]{:S(2)}) copy-start(bf16[512,2048]{1,0:T(8,128)(2,1)} %param.13) | copy-start | bytes 6291460
  6.5 69.0 %all-gather.6.cloned.1.call-start = ((), (), s32[]{:S(2)}) async-start(), calls=%async_computation.2 | async-start | bytes 1179648 | tf_op jit(solution)/shard_map/all_gather | solution.py:24
  11.4 5.8 %copy-start.3 = (bf16[256,4,128]{2,1,0:T(4,128)(2,1)S(1)}, bf16[256,4,128]{2,1,0:T(4,128)(2,1)}, u32[]{:S(2)}) copy-start(bf16[256,4,128]{2,1,0:T(4,128)(2,1)} %param.9) | copy-start | bytes 786436
  11.5 5.8 %copy-start.4 = (bf16[256,4,128]{2,1,0:T(4,128)(2,1)S(1)}, bf16[256,4,128]{2,1,0:T(4,128)(2,1)}, u32[]{:S(2)}) copy-start(bf16[256,4,128]{2,1,0:T(4,128)(2,1)} %param.10) | copy-start | bytes 786436
  12.8 14.3 %copy-start.1 = (f32[4,256,128]{2,0,1:T(4,128)}, f32[4,256,128]{2,0,1:T(4,128)S(1)}, u32[]{:S(2)}) copy-start(f32[4,256,128]{2,0,1:T(4,128)S(1)} %fusion.56) | copy-start | bytes 1572868
  17.2 11.7 %copy-start.7 = (bf16[256,4,128]{2,1,0:T(4,128)(2,1)S(1)}, bf16[256,4,128]{2,1,0:T(4,128)(2,1)}, u32[]{:S(2)}) copy-start(bf16[256,4,128]{2,1,0:T(4,128)(2,1)} %param.8) | copy-start | bytes 786436
  17.2 73.9 %all-gather.8.cloned.1.call-start = ((), (), s32[]{:S(2)}) async-start(), calls=%async_computation.3 | async-start | bytes 1179648 | tf_op jit(solution)/shard_map/all_gather | solution.py:24
  17.3 9.8 %copy-start.6 = (f32[4,256,128]{2,0,1:T(4,128)S(1)}, f32[4,256,128]{2,0,1:T(4,128)}, u32[]{:S(2)}) copy-start(f32[4,256,128]{2,0,1:T(4,128)} %get-tuple-element.213) | copy-start | bytes 1572868
  18.3 12.7 %copy-start.11 = (u32[32]{0:T(128)S(1)}, u32[32]{0:T(128)}, u32[]{:S(2)}) copy-start(u32[32]{0:T(128)} %constant.74) | copy-start | bytes 388
  18.3 41.1 %copy-start.10 = (f32[4,256]{1,0:T(4,128)S(1)}, f32[4,256]{1,0:T(4,128)}, u32[]{:S(2)}) copy-start(f32[4,256]{1,0:T(4,128)} %param.12) | copy-start | bytes 12292
  19.1 43.5 %collective-permute-start = (bf16[2,256,4,128]{3,1,2,0:T(8,128)(2,1)}, bf16[2,256,4,128]{3,1,2,0:T(8,128)(2,1)}, u32[]{:S(2)}, u32[]{:S(2)}) collective-permute-start(bf16[2,256,4,128]{3,1,2,0:T(8,128)(2,1)} %pad_maximum_fusion), channel_id=1, source_target_pairs={{0,16},{4,20},{8,24},{12,28},{1,17},{5,21},{9,25},{13,29},{2,18},{... | collective-permute-start | bytes 1572872 | tf_op jit(solution)/shard_map/ppermute | solution.py:18
  20.4 47.1 %collective-permute-start.1 = (bf16[2,256,4,128]{3,1,2,0:T(8,128)(2,1)}, bf16[2,256,4,128]{3,1,2,0:T(8,128)(2,1)}, u32[]{:S(2)}, u32[]{:S(2)}) collective-permute-start(bf16[2,256,4,128]{3,1,2,0:T(8,128)(2,1)} %pad_maximum_fusion), channel_id=1, source_target_pairs={{0,12},{4,16},{8,20},{12,24},{16,28},{1,13},{5,17},{9,21},{13,25},... | collective-permute-start | bytes 1572872 | tf_op jit(solution)/shard_map/ppermute | solution.py:18
  23.2 45.3 %collective-permute-start.2 = (bf16[2,256,4,128]{3,1,2,0:T(8,128)(2,1)}, bf16[2,256,4,128]{3,1,2,0:T(8,128)(2,1)}, u32[]{:S(2)}, u32[]{:S(2)}) collective-permute-start(bf16[2,256,4,128]{3,1,2,0:T(8,128)(2,1)} %pad_maximum_fusion), channel_id=1, source_target_pairs={{0,8},{4,12},{8,16},{12,20},{16,24},{20,28},{1,9},{5,13},{9,17},{1... | collective-permute-start | bytes 1572872 | tf_op jit(solution)/shard_map/ppermute | solution.py:18
  25.2 44.5 %collective-permute-start.3 = (bf16[2,256,4,128]{3,1,2,0:T(8,128)(2,1)}, bf16[2,256,4,128]{3,1,2,0:T(8,128)(2,1)}, u32[]{:S(2)}, u32[]{:S(2)}) collective-permute-start(bf16[2,256,4,128]{3,1,2,0:T(8,128)(2,1)} %pad_maximum_fusion), channel_id=1, source_target_pairs={{0,4},{4,8},{8,12},{12,16},{16,20},{20,24},{24,28},{1,5},{5,9},{9,... | collective-permute-start | bytes 1572872 | tf_op jit(solution)/shard_map/ppermute | solution.py:18
  28.8 130.2 %reduce-scatter.2.cloned.1.call-start = ((), (), s32[]{:S(2)}) async-start(), calls=%async_computation.1 | async-start | bytes 1310720 | tf_op jit(solution)/shard_map/reduce_scatter | solution.py:172
  101.1 2.9 %copy-start.2 = (f32[4,256,128]{2,0,1:T(4,128)S(1)}, f32[4,256,128]{2,0,1:T(4,128)}, u32[]{:S(2)}) copy-start(f32[4,256,128]{2,0,1:T(4,128)} %copy-done.1) | copy-start | bytes 1572868
  121.4 1.9 %copy-start.5 = (bf16[256,4,128]{2,1,0:T(4,128)(2,1)S(1)}, bf16[256,4,128]{2,1,0:T(4,128)(2,1)}, u32[]{:S(2)}) copy-start(bf16[256,4,128]{2,1,0:T(4,128)(2,1)} %param.10) | copy-start | bytes 786436
  122.7 1.4 copy-start.8
  122.7 1.4 copy-start.9
Sparse Core Ops, SparseCore 0:
  17.3 48.1 all-gather.5
  67.4 23.6 all-gather.7
  131.7 27.3 reduce-scatter.1
where the time goes:
time: 168 us; the launch traced here: 166 us
  waiting for transfers between devices  46.8 us (28%)
  matrix products  39.2 us (23%)
  blocking collectives  25.5 us (15%)
  other arithmetic  20.3 us (12%)
  between operations  14.3 us (9%)
  local copies, waits for them, and re-layouts  11 us (7%)
  starting transfers between devices  8.05 us (5%)
    reduce_scatter x1, waiting for transfers between devices, on_device(): lax.psum_scatter(jnp.dot(flat_local, out_weight, preferred_element_type=j...  27.5 us
    unnamed x1, blocking collectives  25.5 us
    all_gather x2, waiting for transfers between devices, carried_in(): lax.all_gather(part.astype(kind), axis)  15.6 us
    dot_general x6, matrix products, group_step(): jnp.einsum('htf,hsf->hts', direction, key_part, precision=highest)  9.99 us
    dot_general x6, matrix products, group_step(): jnp.einsum('hts,hse->hte', mixing * operator_correlation, key_part, preci...  8.9 us
    select_n x8, other arithmetic, hop(): return jax.tree.map(lambda a, b: jnp.where(reached, a, b), new, before)  8.88 us
    ppermute x4, starting transfers between devices, shifted(): return lax.ppermute(x, axis, pairs)  7.96 us
    dot_general x1, matrix products, window_attention(): jnp.einsum('hqk,khe->qhe', weights, value_rows, preferred_element_type=jn...  4.76 us
  transfers between devices with their start and end apart: 7, of which 3 were waited for; matrix products, arithmetic and copies ran while one was open for 12% of the time, Pallas kernels for 0%

commit v1 on v0

v1 whole, which is shorter than its diff:
```python
import functools

import jax
import jax.numpy as jnp
from jax import lax
from jax.experimental import pallas as pl
from jax.experimental.pallas import tpu as pltpu
from jax.sharding import PartitionSpec as P

WINDOW = 1024
CG_STEPS = 6
RIDGE = 0.25
TINY = 1e-30
LOW = -1e30
MESH = pl.DeviceIdType.MESH
F32 = jnp.float32
BF16 = jnp.bfloat16


def dot(a, b):
    return lax.dot_general(a, b, (((1,), (0,)), ((), ())), preferred_element_type=F32)


def dot_t(a, b):
    return lax.dot_general(a, b, (((1,), (1,)), ((), ())), preferred_element_type=F32)


def dot_tl(a, b):
    return lax.dot_general(a, b, (((0,), (0,)), ((), ())), preferred_element_type=F32)


def split(x):
    hi = x.astype(BF16)
    return hi, (x - hi.astype(F32)).astype(BF16)


def kernel(
    n, nz, back,
    qkv_ref, fs_ref, w_hbm, out_ref,
    kv, qb, fs, st, stl, w, kk, mix, sk, sv, xs, rs, ds, nrm, att, hout, hother, rsend, lsend, rrecv, lrecv,
    w_sem, kv_s, kv_r, sib_s, q_r, fs_s, fs_r, st_s, st_r, h_sem, rs_s, rs_r, ls_s, ls_r,
):
    me = lax.axis_index("seq")
    z = lax.axis_index("head")
    chip, core = me // 2, me % 2
    sib = chip * 2 + (1 - core)
    chips = n // 2
    window = 2 * back
    half, tok, width = kv.shape[2], kv.shape[3], kv.shape[4]
    far_max = max(n - 2 * (back + 1), 0)

    def dev(s, h):
        return (s, h)

    w_copy = pltpu.make_async_copy(w_hbm, w, w_sem)
    w_copy.start()

    barrier = pltpu.get_barrier_semaphore()
    for k in range(1, n):
        pl.semaphore_signal(barrier, inc=1, device_id=dev((me + k) % n, z), device_id_type=MESH)
    for k in range(1, nz):
        pl.semaphore_signal(barrier, inc=1, device_id=dev(me, (z + k) % nz), device_id_type=MESH)
    pl.semaphore_wait(barrier, n - 1 + nz - 1)

    def remote(src, dst, s_sem, r_sem, s, h):
        return pltpu.make_async_remote_copy(
            src_ref=src, dst_ref=dst, send_sem=s_sem, recv_sem=r_sem,
            device_id=dev(s, h), device_id_type=MESH)

    def fs_copy(j, owner):
        return remote(fs_ref.at[j % 2], fs.at[owner], fs_s.at[j], fs_r.at[owner], j, z)

    for j in range(n):
        @pl.when((j // 2 >= chip) & (j != me))
        def _():
            fs_copy(j, me).start()

    def sib_copies():
        other = 1 - core
        return (
            remote(qkv_ref.at[other, pl.ds(1, 2)], kv.at[window + core], sib_s.at[0], kv_r.at[window + core], sib, z),
            remote(qkv_ref.at[other, 0], qb.at[core], sib_s.at[1], q_r, sib, z),
        )

    for c in sib_copies():
        c.start()

    def halo_copy(d, h, slot):
        return remote(qkv_ref.at[h, pl.ds(1, 2)], kv.at[slot], kv_s.at[d - 1, h], kv_r.at[slot],
                      (chip + d) * 2 + h, z)

    for d in range(1, back + 1):
        @pl.when(chip + d < chips)
        def _():
            for h in range(2):
                halo_copy(d, h, window - 2 * d + core).start()

    row = lax.broadcasted_iota(jnp.int32, (tok, tok), 0)
    col = lax.broadcasted_iota(jnp.int32, (tok, tok), 1)
    tri = row >= col
    eye = row == col

    def to_col(r):
        return jnp.sum(jnp.where(eye, jnp.broadcast_to(r, (tok, tok)), 0.0), axis=1, keepdims=True)

    def to_row(c):
        return jnp.sum(jnp.where(eye, jnp.broadcast_to(c, (tok, tok)), 0.0), axis=0, keepdims=True)

    def sums_col(r):
        return jnp.sum(jnp.where(tri, jnp.broadcast_to(r, (tok, tok)), 0.0), axis=1, keepdims=True)

    def inv_norm(x):
        x = x.astype(F32)
        return lax.rsqrt(jnp.sum(x * x, axis=-1, keepdims=True) + 1e-6)

    def local_state(k, v, f, s):
        tail = jnp.exp(jnp.sum(f, axis=1, keepdims=True) - sums_col(f)) * to_col(s)
        r = inv_norm(k)
        wk = (tail * r) * k.astype(F32)
        h0, l0 = split(wk * r)
        h1, l1 = split(wk)
        key = dot_tl(h0, k) + dot_tl(l0, k)
        val = dot_tl(h1, v) + dot_tl(l1, v)
        return key, val

    def st_copy(j, owner):
        return remote(stl.at[j % 2], st.at[owner], st_s.at[j], st_r.at[owner], j, z)

    if far_max > 0:
        @pl.when(chip + back + 1 < chips)
        def _():
            for g in range(2):
                for h in range(half):
                    a, b = local_state(qkv_ref[g, 1, h], qkv_ref[g, 2, h],
                                       fs_ref[g, h:h + 1, :], fs_ref[g, half + h:half + h + 1, :])
                    stl[g, 0, h] = a.astype(BF16)
                    stl[g, 1, h] = b.astype(BF16)
            for j in range(2 * (back + 1), n):
                @pl.when(j // 2 > chip + back)
                def _():
                    st_copy(j, me).start()

    kv[window + core] = qkv_ref[core, 1:3]
    qb[core] = qkv_ref[core, 0]
    fs[me] = fs_ref[core]

    for c in sib_copies():
        c.wait_send()
    remote(qkv_ref.at[0, pl.ds(1, 2)], kv.at[window + 1 - core], sib_s.at[0], kv_r.at[window + 1 - core], sib, z).wait_recv()
    remote(qkv_ref.at[0, 0], qb.at[1 - core], sib_s.at[1], q_r, sib, z).wait_recv()
    for j in range(n):
        @pl.when((j // 2 <= chip) & (j != me))
        def _():
            fs_copy(me, j).wait_recv()

        @pl.when((j // 2 >= chip) & (j != me))
        def _():
            fs_copy(j, me).wait_send()

    def gates(shard, h):
        at = (shard + n) % n
        both = fs[at]
        return both[h:h + 1, :], both[half + h:half + h + 1, :]

    for b in range(2):
        for h in range(half):
            i = b * half + h
            f, s = gates(chip * 2 + b, h)
            k = kv[window + b, 0, h]
            c_col = sums_col(f)
            c_row = to_row(c_col)
            r_row = to_row(inv_norm(k))
            mix[i] = jnp.where(tri, jnp.exp(jnp.minimum(c_col - c_row, 0.0)), 0.0) * (s * r_row * r_row)
            kk[i] = jnp.concatenate((k, k), axis=1)
            nrm[i] = jnp.broadcast_to(1.0 / r_row, (8, tok))
            q = qb[b, h].astype(F32)
            ds[i] = q * lax.rsqrt(jnp.sum(q * q, axis=-1, keepdims=True) + 1e-6)
            rs[i] = ds[i]
            xs[i] = jnp.zeros((tok, width), F32)

    for d in range(back, 0, -1):
        for g in range(2):
            slot = window - 2 * d + g

            @pl.when(chip >= d)
            def _():
                remote(qkv_ref.at[0, pl.ds(1, 2)], kv.at[slot], kv_s.at[0, 0], kv_r.at[slot], me, z).wait_recv()

            @pl.when(chip < d)
            def _():
                kv[slot] = jnp.zeros((2, half, tok, width), BF16)

    for j in range(far_max):
        @pl.when(j // 2 < chip - back)
        def _():
            remote(stl.at[0], st.at[j], st_s.at[0], st_r.at[j], me, z).wait_recv()

    for h in range(half):
        key = jnp.zeros((width, width), F32)
        val = jnp.zeros((width, width), F32)
        for j in range(far_max):
            ok = j // 2 < chip - back
            f, s = gates(j, h)
            e = jnp.exp(jnp.sum(f, axis=1, keepdims=True))
            key = jnp.where(ok, e * key + st[j, 0, h].astype(F32), key)
            val = jnp.where(ok, e * val + st[j, 1, h].astype(F32), val)
        for j in range(window + 1):
            ok = chip * 2 + j >= window
            f, s = gates(chip * 2 - window + j, h)
            if j == window:
                sk[h, 0], sk[h, 1] = split(key)
                sv[h, 0], sv[h, 1] = split(val)
            a, b = local_state(kv[j, 0, h], kv[j, 1, h], f, s)
            e = jnp.exp(jnp.sum(f, axis=1, keepdims=True))
            key = jnp.where(ok, e * key + a, key)
            val = jnp.where(ok, e * val + b, val)
        sk[half + h, 0], sk[half + h, 1] = split(key)
        sv[half + h, 0], sv[half + h, 1] = split(val)

    scale = width ** (-0.5)
    for b in range(2):
        for h in range(half):
            q = qb[b, h]
            parts = []
            for j in range(window + 1):
                sc = dot_t(q, kv[b + j, 0, h]) * scale
                ok = chip * 2 + b + j >= window
                if j == 0:
                    sc = jnp.where((col > row) & ok, sc, LOW)
                elif j == window:
                    sc = jnp.where(tri, sc, LOW)
                else:
                    sc = jnp.where(ok, sc, LOW)
                parts.append(sc)
            top = functools.reduce(jnp.maximum, parts)
            top = jnp.max(top, axis=1, keepdims=True)
            total = jnp.zeros((tok, tok), F32)
            acc = jnp.zeros((tok, width), F32)
            for j in range(window + 1):
                e = jnp.exp(parts[j] - top)
                total = total + e
                acc = acc + dot(e.astype(BF16), kv[b + j, 1, h])
            att[b * half + h] = acc / jnp.sum(total, axis=1, keepdims=True)

    chains = 2 * half

    def carried(i, dh, dl, ref):
        hi, lo = ref[i, 0], ref[i, 1]
        return dot(dh, hi) + dot(dl, hi) + dot(dh, lo)

    leads = []
    for b in range(2):
        for h in range(half):
            f, s = gates(chip * 2 + b, h)
            leads.append(jnp.exp(sums_col(f)))

    def step(_, carry):
        norms = []
        for i in range(chains):
            now = carry[i]
            dirn = ds[i]
            dh, dl = split(dirn)
            corr = dot_t(jnp.concatenate((dh, dl), axis=1), kk[i])
            ph, plo = split(mix[i] * corr)
            k = kk[i][:, :width]
            image = leads[i] * carried(i, dh, dl, sk) + (dot(ph, k) + dot(plo, k)) + RIDGE * dirn
            alpha = now / jnp.maximum(jnp.sum(dirn * image, axis=-1, keepdims=True), TINY)
            xs[i] = xs[i] + alpha * dirn
            res = rs[i] - alpha * image
            rs[i] = res
            new = jnp.sum(res * res, axis=-1, keepdims=True)
            ds[i] = res + (new / jnp.maximum(now, TINY)) * dirn
            norms.append(new)
        return tuple(norms)

    start = tuple(jnp.sum(ds[i] * ds[i], axis=-1, keepdims=True) for i in range(chains))
    lax.fori_loop(0, CG_STEPS, step, start)

    for b in range(2):
        for h in range(half):
            i = b * half + h
            xh, xl = split(xs[i])
            corr = dot_t(jnp.concatenate((xh, xl), axis=1), kk[i])
            ph, plo = split((mix[i] * nrm[i][0:1, :]) * corr)
            v = kv[window + b, 1, h]
            mesa = leads[i] * carried(i, xh, xl, sv) + (dot(ph, v) + dot(plo, v))
            hout[b, :, h * width:(h + 1) * width] = (att[i] + mesa).astype(BF16)

    swap = remote(hout.at[1 - core], hother, h_sem.at[0], h_sem.at[1], sib, z)
    swap.start()
    w_copy.wait()
    swap.wait()

    chunk = tok // nz
    rows = half * width

    def partial(d):
        own = hout[core, d * chunk:(d + 1) * chunk, :]
        other = hother[d * chunk:(d + 1) * chunk, :]
        return dot(own, w[core]) + dot(other, w[1 - core])

    def right(d):
        return remote(rsend.at[d], rrecv.at[d], rs_s.at[d], rs_r.at[d], me, (z + 1) % nz)

    def left(d):
        return remote(lsend.at[d], lrecv.at[d], ls_s.at[d], ls_r.at[d], me, (z + nz - 1) % nz)

    for k in range(nz - 1):
        d = nz - 1 - k

        @pl.when(z < d)
        def _():
            rsend[d] = partial(d).astype(BF16)

            @pl.when(z > 0)
            def _():
                right(d).wait_recv()
                rsend[d] = (rsend[d].astype(F32) + rrecv[d].astype(F32)).astype(BF16)

            right(d).start()

        e = k

        @pl.when(z > e)
        def _():
            lsend[e] = partial(e).astype(BF16)

            @pl.when(z < nz - 1)
            def _():
                left(e).wait_recv()
                lsend[e] = (lsend[e].astype(F32) + lrecv[e].astype(F32)).astype(BF16)

            left(e).start()

    for d in range(nz):
        @pl.when(z == d)
        def _():
            total = partial(d)
            if d > 0:
                right(d).wait_recv()
                total = total + rrecv[d].astype(F32)
            if d < nz - 1:
                left(d).wait_recv()
                total = total + lrecv[d].astype(F32)
            out_ref[...] = total.astype(BF16)

    for d in range(nz):
        @pl.when(z < d)
        def _():
            right(d).wait_send()

        @pl.when(z > d)
        def _():
            left(d).wait_send()

    for d in range(1, back + 1):
        @pl.when(chip + d < chips)
        def _():
            for h in range(2):
                halo_copy(d, h, window - 2 * d + core).wait_send()
    if far_max > 0:
        for j in range(2 * (back + 1), n):
            @pl.when(j // 2 > chip + back)
            def _():
                st_copy(j, me).wait_send()


def on_device(queries, keys, values, log_forget, strength, out_weight):
    tok, heads, width = queries.shape
    n, nz = lax.axis_size("seq"), lax.axis_size("head")
    half = heads // 2
    back = max(WINDOW // (2 * tok), 1)
    qkv = jnp.stack((queries, keys, values)).reshape(3, tok, 2, half, width)
    qkv = jnp.transpose(qkv, (2, 0, 3, 1, 4))
    fs = jnp.concatenate((log_forget.reshape(2, half, tok), strength.reshape(2, half, tok)), axis=1)
    model = out_weight.shape[1]
    weight = out_weight.reshape(2, half * width, model)
    chunk = tok // nz
    slots = 2 * back + 2
    chains = 2 * half
    far = max(n - 2 * (back + 1), 1)
    dma = pltpu.SemaphoreType.DMA
    vmem = pl.BlockSpec(memory_space=pltpu.VMEM)
    return pl.pallas_call(
        functools.partial(kernel, n, nz, back),
        out_shape=jax.ShapeDtypeStruct((chunk, model), BF16),
        in_specs=[vmem, vmem, pl.BlockSpec(memory_space=pl.ANY)],
        out_specs=vmem,
        scratch_shapes=[
            pltpu.VMEM((slots, 2, half, tok, width), BF16),
            pltpu.VMEM((2, half, tok, width), BF16),
            pltpu.VMEM((n, 2 * half, tok), F32),
            pltpu.VMEM((far, 2, half, width, width), BF16),
            pltpu.VMEM((2, 2, half, width, width), BF16),
            pltpu.VMEM((2, half * width, model), BF16),
            pltpu.VMEM((chains, tok, 2 * width), BF16),
            pltpu.VMEM((chains, tok, tok), F32),
            pltpu.VMEM((chains, 2, width, width), BF16),
            pltpu.VMEM((chains, 2, width, width), BF16),
            pltpu.VMEM((chains, tok, width), F32),
            pltpu.VMEM((chains, tok, width), F32),
            pltpu.VMEM((chains, tok, width), F32),
            pltpu.VMEM((chains, 8, tok), F32),
            pltpu.VMEM((chains, tok, width), F32),
            pltpu.VMEM((2, tok, half * width), BF16),
            pltpu.VMEM((tok, half * width), BF16),
            pltpu.VMEM((nz, chunk, model), BF16),
            pltpu.VMEM((nz, chunk, model), BF16),
            pltpu.VMEM((nz, chunk, model), BF16),
            pltpu.VMEM((nz, chunk, model), BF16),
            dma(()),
            dma((back, 2)), dma((slots,)), dma((2,)), dma(()), dma((n,)), dma((n,)),
            dma((n,)), dma((n,)), dma((2,)), dma((nz,)), dma((nz,)), dma((nz,)), dma((nz,)),
        ],
        compiler_params=pltpu.CompilerParams(
            collective_id=0, has_side_effects=True, vmem_limit_bytes=56 * 1024 * 1024),
    )(qkv, fs, weight)


def solution(mesh):
    in_specs = (
        P("seq", "head", None),
        P("seq", "head", None),
        P("seq", "head", None),
        P("head", "seq"),
        P("head", "seq"),
        P("head", None),
    )
    return jax.shard_map(
        on_device, mesh=mesh, in_specs=in_specs, out_specs=P(("seq", "head"), None), check_vma=False)
```

time: 168 us -> 79.7 us (0.47); the launches traced: 166 us -> 79.5 us
  Pallas kernels: 0 us -> 73.2 us
  waiting for transfers between devices: 46.8 us -> 0 us
  matrix products: 39.2 us -> 0 us
  blocking collectives: 25.5 us -> 0 us
  other arithmetic: 20.3 us -> 1.57 us
  between operations: 14.3 us -> 0.02 us
  starting transfers between devices: 8.05 us -> 0 us
  local copies, waits for them, and re-layouts: 11 us -> 4.7 us
    pallas_call x0 -> x1, Pallas kernels: none -> 73.2 us  [on_device(): pl.pallas_call(functools.partial(kernel, n, nz, back), out_shape=jax.Shap...]
    dot_general x25 -> x0, matrix products: 36 us -> none  [the longest x6 9.99 us: group_step(): jnp.einsum('htf,hsf->hts', direction, key_part, precision=highest)]
    reduce_scatter x1 -> x0, waiting for transfers between devices: 27.5 us -> none  [on_device(): lax.psum_scatter(jnp.dot(flat_local, out_weight, preferred_element_type=j...]
    unnamed x1 -> x0, blocking collectives: 25.5 us -> none
    all_gather x2 -> x0, waiting for transfers between devices: 15.6 us -> none  [carried_in(): lax.all_gather(part.astype(kind), axis)]
    select_n x8 -> x0, other arithmetic: 8.88 us -> none  [hop(): return jax.tree.map(lambda a, b: jnp.where(reached, a, b), new, before)]
    ppermute x4 -> x0, starting transfers between devices: 7.96 us -> none  [shifted(): return lax.ppermute(x, axis, pairs)]
    ppermute x4 -> x0, waiting for transfers between devices: 3.73 us -> none  [shifted(): return lax.ppermute(x, axis, pairs)]
  transfers between devices with their start and end apart: 7 -> 0, of which waited for: 3 -> 0; matrix products, arithmetic and copies ran while one was open for 12% -> 0% of each run, Pallas kernels for 0% -> 0%
where the time goes in v1:
time: 79.7 us; the launch traced here: 79.5 us
  Pallas kernels  73.2 us (92%)
  local copies, waits for them, and re-layouts  4.7 us (6%)
  other arithmetic  1.57 us (2%)
    pallas_call x1, Pallas kernels, on_device(): pl.pallas_call(functools.partial(kernel, n, nz, back), out_shape=jax.Shap...  73.2 us
    unnamed x8, local copies, waits for them, and re-layouts  4.67 us

profile of v1, /device:TPU:4, one launch (start us, length us, event | category | flops | bytes accessed | tf_op | source)
XLA Modules:
  0.0 79.5 jit_solution(12709841267958207432)
XLA Ops:
  0.0 0.0 copy-start
  0.0 0.0 copy-start.1
  0.0 1.0 %copy.7 = bf16[256,4,128]{2,0,1:T(8,128)(2,1)S(1)} copy(bf16[256,4,128]{2,1,0:T(4,128)(2,1)} %param.6) | data formatting | bytes 524288 | tf_op args[0]
  1.0 1.0 %copy.8 = bf16[256,4,128]{2,0,1:T(8,128)(2,1)S(1)} copy(bf16[256,4,128]{2,1,0:T(4,128)(2,1)} %param.7) | data formatting | bytes 524288 | tf_op args[1]
  2.0 1.0 %copy.9 = bf16[256,4,128]{2,0,1:T(8,128)(2,1)S(1)} copy(bf16[256,4,128]{2,1,0:T(4,128)(2,1)} %param.8) | data formatting | bytes 524288 | tf_op args[2]
  3.0 1.0 %maximum_bitcast_fusion.qkv_ref = bf16[2,3,2,256,128]{4,3,2,1,0:T(8,128)(2,1)} fusion(bf16[1,256,2,2,128]{4,1,3,0,2:T(8,128)(2,1)S(1)} %bitcast.9, bf16[1,256,2,2,128]{4,1,3,0,2:T(8,128)(2,1)S(1)} %bitcast.8, bf16[1,256,2,2,128]{4,1,3,0,2:T(8,128)(2,1)S(1)} %bitcast.7), kind=kLoop, calls=%fused_computation | loop fusion | flops 786432 | bytes 1572864 | tf_op jit(solution)/shard_map/transpose | solution.py:374
  4.0 0.0 copy-done
  4.0 0.0 copy-done.1
  4.0 0.6 pad_maximum_fusion.fs_ref
  4.6 73.2 %shard_map.64 = bf16[64,2048]{1,0:T(8,128)(2,1)} custom-call(bf16[2,3,2,256,128]{4,3,2,1,0:T(8,128)(2,1)} %maximum_bitcast_fusion.qkv_ref, f32[2,4,256]{2,1,0:T(4,128)} %pad_maximum_fusion.fs_ref, bf16[2,256,2048]{2,1,0:T(8,128)(2,1)} %bitcast.6), custom_call_target="tpu_custom_call" | custom-call | tf_op jit(solution)/shard_map/pallas_call | solution.py:384
  77.8 1.7 %copy.11 = bf16[64,2048]{1,0:T(8,128)(2,1)} copy(bf16[64,2048]{1,0:T(8,128)(2,1)} %shard_map.64) | data formatting | bytes 524288
  (2 shorter events, 0.0 us)
Async XLA Ops:
  0.0 4.0 %copy-start = (f32[4,256]{1,0:T(4,128)S(1)}, f32[4,256]{1,0:T(4,128)}, u32[]{:S(2)}) copy-start(f32[4,256]{1,0:T(4,128)} %param.9) | copy-start | bytes 12292
  0.0 4.0 %copy-start.1 = (f32[4,256]{1,0:T(4,128)S(1)}, f32[4,256]{1,0:T(4,128)}, u32[]{:S(2)}) copy-start(f32[4,256]{1,0:T(4,128)} %param.10) | copy-start | bytes 12292

commit v2 on v1

--- a/solution.py
+++ b/solution.py
@@ -38,7 +38,7 @@
     n, nz, back,
     qkv_ref, fs_ref, w_hbm, out_ref,
     kv, qb, fs, st, stl, w, kk, mix, sk, sv, xs, rs, ds, nrm, att, hout, hother, rsend, lsend, rrecv, lrecv,
-    w_sem, kv_s, kv_r, sib_s, q_r, fs_s, fs_r, st_s, st_r, h_sem, rs_s, rs_r, ls_s, ls_r,
+    w_sem, kv_s, kv_r, sib_s, q_r, fs_s, fs_r, st_s, st_r, rl_s, h_sem, rs_s, rs_r, ls_s, ls_r,
 ):
     me = lax.axis_index("seq")
     z = lax.axis_index("head")
@@ -48,6 +48,7 @@
     window = 2 * back
     half, tok, width = kv.shape[2], kv.shape[3], kv.shape[4]
     far_max = max(n - 2 * (back + 1), 0)
+    relay = chips == 4 and back == 2
 
     def dev(s, h):
         return (s, h)
@@ -78,22 +79,32 @@
     def sib_copies():
         other = 1 - core
         return (
-            remote(qkv_ref.at[other, pl.ds(1, 2)], kv.at[window + core], sib_s.at[0], kv_r.at[window + core], sib, z),
+            remote(qkv_ref.at[other, pl.ds(1, 2)], kv.at[window + core], sib_s.at[0], kv_r.at[window + core, 0], sib, z),
             remote(qkv_ref.at[other, 0], qb.at[core], sib_s.at[1], q_r, sib, z),
         )
 
     for c in sib_copies():
         c.start()
 
-    def halo_copy(d, h, slot):
-        return remote(qkv_ref.at[h, pl.ds(1, 2)], kv.at[slot], kv_s.at[d - 1, h], kv_r.at[slot],
+    def halo_copy(d, h, slot, part):
+        return remote(qkv_ref.at[h, 1 + part], kv.at[slot, part], kv_s.at[d - 1, h, part], kv_r.at[slot, part],
                       (chip + d) * 2 + h, z)
 
-    for d in range(1, back + 1):
-        @pl.when(chip + d < chips)
-        def _():
-            for h in range(2):
-                halo_copy(d, h, window - 2 * d + core).start()
+    def halo_each(part, act):
+        for d in range(back, 0, -1):
+            ok = chip + d < chips
+            if relay and part == 0 and d == 1:
+                ok = ok & (chip != 1)
+
+            @pl.when(ok)
+            def _():
+                for h in range(2):
+                    act(halo_copy(d, h, window - 2 * d + core, part))
+
+    def relay_copy(g):
+        return remote(kv.at[g, 0], kv.at[window - 2 + g, 0], rl_s.at[g], kv_r.at[window - 2 + g, 0], me - 2, z)
+
+    halo_each(0, lambda c: c.start())
 
     row = lax.broadcasted_iota(jnp.int32, (tok, tok), 0)
     col = lax.broadcasted_iota(jnp.int32, (tok, tok), 1)
@@ -113,14 +124,17 @@
         x = x.astype(F32)
         return lax.rsqrt(jnp.sum(x * x, axis=-1, keepdims=True) + 1e-6)
 
-    def local_state(k, v, f, s):
+    def local_state(k, v, f, s, key_too, val_too):
         tail = jnp.exp(jnp.sum(f, axis=1, keepdims=True) - sums_col(f)) * to_col(s)
         r = inv_norm(k)
         wk = (tail * r) * k.astype(F32)
-        h0, l0 = split(wk * r)
-        h1, l1 = split(wk)
-        key = dot_tl(h0, k) + dot_tl(l0, k)
-        val = dot_tl(h1, v) + dot_tl(l1, v)
+        key = val = None
+        if key_too:
+            h0, l0 = split(wk * r)
+            key = dot_tl(h0, k) + dot_tl(l0, k)
+        if val_too:
+            h1, l1 = split(wk)
+            val = dot_tl(h1, v) + dot_tl(l1, v)
         return key, val
 
     def st_copy(j, owner):
@@ -132,7 +146,7 @@
             for g in range(2):
                 for h in range(half):
                     a, b = local_state(qkv_ref[g, 1, h], qkv_ref[g, 2, h],
-                                       fs_ref[g, h:h + 1, :], fs_ref[g, half + h:half + h + 1, :])
+                                       fs_ref[g, h:h + 1, :], fs_ref[g, half + h:half + h + 1, :], True, True)
                     stl[g, 0, h] = a.astype(BF16)
                     stl[g, 1, h] = b.astype(BF16)
             for j in range(2 * (back + 1), n):
@@ -140,13 +154,15 @@
                 def _():
                     st_copy(j, me).start()
 
+    halo_each(1, lambda c: c.start())
+
     kv[window + core] = qkv_ref[core, 1:3]
     qb[core] = qkv_ref[core, 0]
     fs[me] = fs_ref[core]
 
     for c in sib_copies():
         c.wait_send()
-    remote(qkv_ref.at[0, pl.ds(1, 2)], kv.at[window + 1 - core], sib_s.at[0], kv_r.at[window + 1 - core], sib, z).wait_recv()
+    remote(qkv_ref.at[0, pl.ds(1, 2)], kv.at[window + 1 - core], sib_s.at[0], kv_r.at[window + 1 - core, 0], sib, z).wait_recv()
     remote(qkv_ref.at[0, 0], qb.at[1 - core], sib_s.at[1], q_r, sib, z).wait_recv()
     for j in range(n):
         @pl.when((j // 2 <= chip) & (j != me))
@@ -178,44 +194,84 @@
             rs[i] = ds[i]
             xs[i] = jnp.zeros((tok, width), F32)
 
-    for d in range(back, 0, -1):
-        for g in range(2):
-            slot = window - 2 * d + g
-
-            @pl.when(chip >= d)
-            def _():
-                remote(qkv_ref.at[0, pl.ds(1, 2)], kv.at[slot], kv_s.at[0, 0], kv_r.at[slot], me, z).wait_recv()
-
-            @pl.when(chip < d)
-            def _():
-                kv[slot] = jnp.zeros((2, half, tok, width), BF16)
-
+    def arrivals(part):
+        for d in range(back, 0, -1):
+            for g in range(2):
+                slot = window - 2 * d + g
+
+                @pl.when(chip >= d)
+                def _():
+                    remote(qkv_ref.at[0, 1], kv.at[slot, part], kv_s.at[0, 0, 0], kv_r.at[slot, part], me, z).wait_recv()
+                    if relay and part == 0 and d == 2:
+                        @pl.when(chip == 3)
+                        def _():
+                            relay_copy(g).start()
+
+                @pl.when(chip < d)
+                def _():
+                    kv[slot, part] = jnp.zeros((half, tok, width), BF16)
+
+    def states(part, out):
+        for h in range(half):
+            acc = jnp.zeros((width, width), F32)
+            for j in range(far_max):
+                ok = j // 2 < chip - back
+                f, s = gates(j, h)
+                e = jnp.exp(jnp.sum(f, axis=1, keepdims=True))
+                acc = jnp.where(ok, e * acc + st[j, part, h].astype(F32), acc)
+            for j in range(window + 1):
+                ok = chip * 2 + j >= window
+                f, s = gates(chip * 2 - window + j, h)
+                if j == window:
+                    out[h, 0], out[h, 1] = split(acc)
+                new = local_state(kv[j, 0, h], kv[j, 1, h] if part else None, f, s, part == 0, part == 1)[part]
+                e = jnp.exp(jnp.sum(f, axis=1, keepdims=True))
+                acc = jnp.where(ok, e * acc + new, acc)
+            out[half + h, 0], out[half + h, 1] = split(acc)
+
+    arrivals(0)
     for j in range(far_max):
         @pl.when(j // 2 < chip - back)
         def _():
             remote(stl.at[0], st.at[j], st_s.at[0], st_r.at[j], me, z).wait_recv()
-
-    for h in range(half):
-        key = jnp.zeros((width, width), F32)
-        val = jnp.zeros((width, width), F32)
-        for j in range(far_max):
-            ok = j // 2 < chip - back
-            f, s = gates(j, h)
-            e = jnp.exp(jnp.sum(f, axis=1, keepdims=True))
-            key = jnp.where(ok, e * key + st[j, 0, h].astype(F32), key)
-            val = jnp.where(ok, e * val + st[j, 1, h].astype(F32), val)
-        for j in range(window + 1):
-            ok = chip * 2 + j >= window
-            f, s = gates(chip * 2 - window + j, h)
-            if j == window:
-                sk[h, 0], sk[h, 1] = split(key)
-                sv[h, 0], sv[h, 1] = split(val)
-            a, b = local_state(kv[j, 0, h], kv[j, 1, h], f, s)
-            e = jnp.exp(jnp.sum(f, axis=1, keepdims=True))
-            key = jnp.where(ok, e * key + a, key)
-            val = jnp.where(ok, e * val + b, val)
-        sk[half + h, 0], sk[half + h, 1] = split(key)
-        sv[half + h, 0], sv[half + h, 1] = split(val)
+    states(0, sk)
+
+    chains = 2 * half
+
+    def carried(i, dh, dl, ref):
+        hi, lo = ref[i, 0], ref[i, 1]
+        return dot(dh, hi) + dot(dl, hi) + dot(dh, lo)
+
+    leads = []
+    for b in range(2):
+        for h in range(half):
+            f, s = gates(chip * 2 + b, h)
+            leads.append(jnp.exp(sums_col(f)))
+
+    def step(_, carry):
+        norms = []
+        for i in range(chains):
+            now = carry[i]
+            dirn = ds[i]
+            dh, dl = split(dirn)
+            corr = dot_t(jnp.concatenate((dh, dl), axis=1), kk[i])
+            ph, plo = split(mix[i] * corr)
+            k = kk[i][:, :width]
+            image = leads[i] * carried(i, dh, dl, sk) + (dot(ph, k) + dot(plo, k)) + RIDGE * dirn
+            alpha = now / jnp.maximum(jnp.sum(dirn * image, axis=-1, keepdims=True), TINY)
+            xs[i] = xs[i] + alpha * dirn
+            res = rs[i] - alpha * image
+            rs[i] = res
+            new = jnp.sum(res * res, axis=-1, keepdims=True)
+            ds[i] = res + (new / jnp.maximum(now, TINY)) * dirn
+            norms.append(new)
+        return tuple(norms)
+
+    start = tuple(jnp.sum(ds[i] * ds[i], axis=-1, keepdims=True) for i in range(chains))
+    lax.fori_loop(0, CG_STEPS, step, start)
+
+    arrivals(1)
+    states(1, sv)
 
     scale = width ** (-0.5)
     for b in range(2):
@@ -242,40 +298,6 @@
                 acc = acc + dot(e.astype(BF16), kv[b + j, 1, h])
             att[b * half + h] = acc / jnp.sum(total, axis=1, keepdims=True)
 
-    chains = 2 * half
-
-    def carried(i, dh, dl, ref):
-        hi, lo = ref[i, 0], ref[i, 1]
-        return dot(dh, hi) + dot(dl, hi) + dot(dh, lo)
-
-    leads = []
-    for b in range(2):
-        for h in range(half):
-            f, s = gates(chip * 2 + b, h)
-            leads.append(jnp.exp(sums_col(f)))
-
-    def step(_, carry):
-        norms = []
-        for i in range(chains):
-            now = carry[i]
-            dirn = ds[i]
-            dh, dl = split(dirn)
-            corr = dot_t(jnp.concatenate((dh, dl), axis=1), kk[i])
-            ph, plo = split(mix[i] * corr)
-            k = kk[i][:, :width]
-            image = leads[i] * carried(i, dh, dl, sk) + (dot(ph, k) + dot(plo, k)) + RIDGE * dirn
-            alpha = now / jnp.maximum(jnp.sum(dirn * image, axis=-1, keepdims=True), TINY)
-            xs[i] = xs[i] + alpha * dirn
-            res = rs[i] - alpha * image
-            rs[i] = res
-            new = jnp.sum(res * res, axis=-1, keepdims=True)
-            ds[i] = res + (new / jnp.maximum(now, TINY)) * dirn
-            norms.append(new)
-        return tuple(norms)
-
-    start = tuple(jnp.sum(ds[i] * ds[i], axis=-1, keepdims=True) for i in range(chains))
-    lax.fori_loop(0, CG_STEPS, step, start)
-
     for b in range(2):
         for h in range(half):
             i = b * half + h
@@ -292,72 +314,87 @@
     swap.wait()
 
     chunk = tok // nz
-    rows = half * width
-
-    def partial(d):
+    pieces = rsend.shape[1]
+    cols = w.shape[2] // pieces
+
+    def at(p):
+        return pl.ds(pl.multiple_of(p * cols, cols), cols)
+
+    def partial(d, p):
         own = hout[core, d * chunk:(d + 1) * chunk, :]
         other = hother[d * chunk:(d + 1) * chunk, :]
-        return dot(own, w[core]) + dot(other, w[1 - core])
-
-    def right(d):
-        return remote(rsend.at[d], rrecv.at[d], rs_s.at[d], rs_r.at[d], me, (z + 1) % nz)
-
-    def left(d):
-        return remote(lsend.at[d], lrecv.at[d], ls_s.at[d], ls_r.at[d], me, (z + nz - 1) % nz)
+        return dot(own, w[core, :, at(p)]) + dot(other, w[1 - core, :, at(p)])
+
+    def right(d, p):
+        return remote(rsend.at[d, p], rrecv.at[d, p], rs_s.at[d, p], rs_r.at[d, p], me, (z + 1) % nz)
+
+    def left(d, p):
+        return remote(lsend.at[d, p], lrecv.at[d, p], ls_s.at[d, p], ls_r.at[d, p], me, (z + nz - 1) % nz)
 
     for k in range(nz - 1):
-        d = nz - 1 - k
-
-        @pl.when(z < d)
-        def _():
-            rsend[d] = partial(d).astype(BF16)
-
-            @pl.when(z > 0)
-            def _():
-                right(d).wait_recv()
-                rsend[d] = (rsend[d].astype(F32) + rrecv[d].astype(F32)).astype(BF16)
-
-            right(d).start()
-
-        e = k
-
-        @pl.when(z > e)
-        def _():
-            lsend[e] = partial(e).astype(BF16)
-
-            @pl.when(z < nz - 1)
-            def _():
-                left(e).wait_recv()
-                lsend[e] = (lsend[e].astype(F32) + lrecv[e].astype(F32)).astype(BF16)
-
-            left(e).start()
+        d, e = nz - 1 - k, k
+
+        @pl.loop(0, pieces)
+        def _(p):
+            @pl.when(z < d)
+            def _():
+                @pl.when(z == 0)
+                def _():
+                    rsend[d, p] = partial(d, p).astype(BF16)
+
+                @pl.when(z > 0)
+                def _():
+                    mine = partial(d, p)
+                    right(d, p).wait_recv()
+                    rsend[d, p] = (mine + rrecv[d, p].astype(F32)).astype(BF16)
+
+                right(d, p).start()
+
+            @pl.when(z > e)
+            def _():
+                @pl.when(z == nz - 1)
+                def _():
+                    lsend[e, p] = partial(e, p).astype(BF16)
+
+                @pl.when(z < nz - 1)
+                def _():
+                    mine = partial(e, p)
+                    left(e, p).wait_recv()
+                    lsend[e, p] = (mine + lrecv[e, p].astype(F32)).astype(BF16)
+
+                left(e, p).start()
 
     for d in range(nz):
         @pl.when(z == d)
         def _():
-            total = partial(d)
-            if d > 0:
-                right(d).wait_recv()
-                total = total + rrecv[d].astype(F32)
-            if d < nz - 1:
-                left(d).wait_recv()
-                total = total + lrecv[d].astype(F32)
-            out_ref[...] = total.astype(BF16)
+            @pl.loop(0, pieces)
+            def _(p):
+                total = partial(d, p)
+                if d > 0:
+                    right(d, p).wait_recv()
+                    total = total + rrecv[d, p].astype(F32)
+                if d < nz - 1:
+                    left(d, p).wait_recv()
+                    total = total + lrecv[d, p].astype(F32)
+                out_ref[:, at(p)] = total.astype(BF16)
 
     for d in range(nz):
-        @pl.when(z < d)
-        def _():
-            right(d).wait_send()
-
-        @pl.when(z > d)
-        def _():
-            left(d).wait_send()
-
-    for d in range(1, back + 1):
-        @pl.when(chip + d < chips)
-        def _():
-            for h in range(2):
-                halo_copy(d, h, window - 2 * d + core).wait_send()
+        for p in range(pieces):
+            @pl.when(z < d)
+            def _():
+                right(d, p).wait_send()
+
+            @pl.when(z > d)
+            def _():
+                left(d, p).wait_send()
+
+    halo_each(0, lambda c: c.wait_send())
+    halo_each(1, lambda c: c.wait_send())
+    if relay:
+        @pl.when(chip == 3)
+        def _():
+            for g in range(2):
+                relay_copy(g).wait_send()
     if far_max > 0:
         for j in range(2 * (back + 1), n):
             @pl.when(j // 2 > chip + back)
@@ -378,6 +415,7 @@
     chunk = tok // nz
     slots = 2 * back + 2
     chains = 2 * half
+    pieces = 4
     far = max(n - 2 * (back + 1), 1)
     dma = pltpu.SemaphoreType.DMA
     vmem = pl.BlockSpec(memory_space=pltpu.VMEM)
@@ -404,13 +442,14 @@
             pltpu.VMEM((chains, tok, width), F32),
             pltpu.VMEM((2, tok, half * width), BF16),
             pltpu.VMEM((tok, half * width), BF16),
-            pltpu.VMEM((nz, chunk, model), BF16),
-            pltpu.VMEM((nz, chunk, model), BF16),
-            pltpu.VMEM((nz, chunk, model), BF16),
-            pltpu.VMEM((nz, chunk, model), BF16),
+            pltpu.VMEM((nz, pieces, chunk, model // pieces), BF16),
+            pltpu.VMEM((nz, pieces, chunk, model // pieces), BF16),
+            pltpu.VMEM((nz, pieces, chunk, model // pieces), BF16),
+            pltpu.VMEM((nz, pieces, chunk, model // pieces), BF16),
             dma(()),
-            dma((back, 2)), dma((slots,)), dma((2,)), dma(()), dma((n,)), dma((n,)),
-            dma((n,)), dma((n,)), dma((2,)), dma((nz,)), dma((nz,)), dma((nz,)), dma((nz,)),
+            dma((back, 2, 2)), dma((slots, 2)), dma((2,)), dma(()), dma((n,)), dma((n,)),
+            dma((n,)), dma((n,)), dma((2,)), dma((2,)),
+            dma((nz, pieces)), dma((nz, pieces)), dma((nz, pieces)), dma((nz, pieces)),
         ],
         compiler_params=pltpu.CompilerParams(
             collective_id=0, has_side_effects=True, vmem_limit_bytes=56 * 1024 * 1024),

time: 79.7 us -> 84 us (1.054); the launches traced: 79.5 us -> 82.5 us
  Pallas kernels: 73.2 us -> 76.3 us
    pallas_call x1, Pallas kernels: 73.2 us -> 76.3 us  [on_device(): pl.pallas_call(functools.partial(kernel, n, nz, back), out_shape=jax.Shap...]
where the time goes in v2:
time: 84 us; the launch traced here: 82.5 us
  Pallas kernels  76.3 us (91%)
  local copies, waits for them, and re-layouts  4.7 us (6%)
  other arithmetic  1.57 us (2%)
    pallas_call x1, Pallas kernels, on_device(): pl.pallas_call(functools.partial(kernel, n, nz, back), out_shape=jax.Shap...  76.3 us
    unnamed x8, local copies, waits for them, and re-layouts  4.67 us

profile of v2, /device:TPU:4, one launch (start us, length us, event | category | flops | bytes accessed | tf_op | source)
XLA Modules:
  0.0 82.5 jit_solution(9014390717615536935)
XLA Ops:
  0.0 0.0 copy-start
  0.0 0.0 copy-start.1
  0.0 1.0 %copy.7 = bf16[256,4,128]{2,0,1:T(8,128)(2,1)S(1)} copy(bf16[256,4,128]{2,1,0:T(4,128)(2,1)} %param.6) | data formatting | bytes 524288 | tf_op args[0]
  1.0 1.0 %copy.8 = bf16[256,4,128]{2,0,1:T(8,128)(2,1)S(1)} copy(bf16[256,4,128]{2,1,0:T(4,128)(2,1)} %param.7) | data formatting | bytes 524288 | tf_op args[1]
  2.0 1.0 %copy.9 = bf16[256,4,128]{2,0,1:T(8,128)(2,1)S(1)} copy(bf16[256,4,128]{2,1,0:T(4,128)(2,1)} %param.8) | data formatting | bytes 524288 | tf_op args[2]
  3.0 1.0 %maximum_bitcast_fusion.qkv_ref = bf16[2,3,2,256,128]{4,3,2,1,0:T(8,128)(2,1)} fusion(bf16[1,256,2,2,128]{4,1,3,0,2:T(8,128)(2,1)S(1)} %bitcast.9, bf16[1,256,2,2,128]{4,1,3,0,2:T(8,128)(2,1)S(1)} %bitcast.8, bf16[1,256,2,2,128]{4,1,3,0,2:T(8,128)(2,1)S(1)} %bitcast.7), kind=kLoop, calls=%fused_computation | loop fusion | flops 786432 | bytes 1572864 | tf_op jit(solution)/shard_map/transpose | solution.py:411
  4.0 0.0 copy-done
  4.0 0.0 copy-done.1
  4.0 0.6 pad_maximum_fusion.fs_ref
  4.6 76.3 %shard_map.64 = bf16[64,2048]{1,0:T(8,128)(2,1)} custom-call(bf16[2,3,2,256,128]{4,3,2,1,0:T(8,128)(2,1)} %maximum_bitcast_fusion.qkv_ref, f32[2,4,256]{2,1,0:T(4,128)} %pad_maximum_fusion.fs_ref, bf16[2,256,2048]{2,1,0:T(8,128)(2,1)} %bitcast.6), custom_call_target="tpu_custom_call" | custom-call | tf_op jit(solution)/shard_map/pallas_call | solution.py:422
  80.9 1.7 %copy.11 = bf16[64,2048]{1,0:T(8,128)(2,1)} copy(bf16[64,2048]{1,0:T(8,128)(2,1)} %shard_map.64) | data formatting | bytes 524288
  (2 shorter events, 0.0 us)
Async XLA Ops:
  0.0 4.0 %copy-start = (f32[4,256]{1,0:T(4,128)S(1)}, f32[4,256]{1,0:T(4,128)}, u32[]{:S(2)}) copy-start(f32[4,256]{1,0:T(4,128)} %param.9) | copy-start | bytes 12292
  0.0 4.0 %copy-start.1 = (f32[4,256]{1,0:T(4,128)S(1)}, f32[4,256]{1,0:T(4,128)}, u32[]{:S(2)}) copy-start(f32[4,256]{1,0:T(4,128)} %param.10) | copy-start | bytes 12292

commit v3 on v2

--- a/solution.py
+++ b/solution.py
@@ -36,8 +36,8 @@
 
 def kernel(
     n, nz, back,
-    qkv_ref, fs_ref, w_hbm, out_ref,
-    kv, qb, fs, st, stl, w, kk, mix, sk, sv, xs, rs, ds, nrm, att, hout, hother, rsend, lsend, rrecv, lrecv,
+    q_ref, k_ref, v_ref, fs_ref, w_hbm, out_ref,
+    kv, qb, fs, st, stl, w, kk, mix, sk, sv, xs, rs, ds, nrm, att, hout, hother, prt, rsend, lsend, rrecv, lrecv,
     w_sem, kv_s, kv_r, sib_s, q_r, fs_s, fs_r, st_s, st_r, rl_s, h_sem, rs_s, rs_r, ls_s, ls_r,
 ):
     me = lax.axis_index("seq")
@@ -79,15 +79,16 @@
     def sib_copies():
         other = 1 - core
         return (
-            remote(qkv_ref.at[other, pl.ds(1, 2)], kv.at[window + core], sib_s.at[0], kv_r.at[window + core, 0], sib, z),
-            remote(qkv_ref.at[other, 0], qb.at[core], sib_s.at[1], q_r, sib, z),
+            remote(k_ref.at[other], kv.at[window + core, 0], sib_s.at[0], kv_r.at[window + core, 0], sib, z),
+            remote(q_ref.at[other], qb.at[core], sib_s.at[1], q_r, sib, z),
+            remote(v_ref.at[other], kv.at[window + core, 1], sib_s.at[2], kv_r.at[window + core, 1], sib, z),
         )
 
     for c in sib_copies():
         c.start()
 
     def halo_copy(d, h, slot, part):
-        return remote(qkv_ref.at[h, 1 + part], kv.at[slot, part], kv_s.at[d - 1, h, part], kv_r.at[slot, part],
+        return remote((k_ref, v_ref)[part].at[h], kv.at[slot, part], kv_s.at[d - 1, h, part], kv_r.at[slot, part],
                       (chip + d) * 2 + h, z)
 
     def halo_each(part, act):
@@ -145,7 +146,7 @@
         def _():
             for g in range(2):
                 for h in range(half):
-                    a, b = local_state(qkv_ref[g, 1, h], qkv_ref[g, 2, h],
+                    a, b = local_state(k_ref[g, h], v_ref[g, h],
                                        fs_ref[g, h:h + 1, :], fs_ref[g, half + h:half + h + 1, :], True, True)
                     stl[g, 0, h] = a.astype(BF16)
                     stl[g, 1, h] = b.astype(BF16)
@@ -156,14 +157,16 @@
 
     halo_each(1, lambda c: c.start())
 
-    kv[window + core] = qkv_ref[core, 1:3]
-    qb[core] = qkv_ref[core, 0]
+    kv[window + core, 0] = k_ref[core]
+    kv[window + core, 1] = v_ref[core]
+    qb[core] = q_ref[core]
     fs[me] = fs_ref[core]
 
     for c in sib_copies():
         c.wait_send()
-    remote(qkv_ref.at[0, pl.ds(1, 2)], kv.at[window + 1 - core], sib_s.at[0], kv_r.at[window + 1 - core, 0], sib, z).wait_recv()
-    remote(qkv_ref.at[0, 0], qb.at[1 - core], sib_s.at[1], q_r, sib, z).wait_recv()
+    for part in range(2):
+        remote(k_ref.at[0], kv.at[window + 1 - core, part], sib_s.at[0], kv_r.at[window + 1 - core, part], sib, z).wait_recv()
+    remote(q_ref.at[0], qb.at[1 - core], sib_s.at[1], q_r, sib, z).wait_recv()
     for j in range(n):
         @pl.when((j // 2 <= chip) & (j != me))
         def _():
@@ -201,7 +204,7 @@
 
                 @pl.when(chip >= d)
                 def _():
-                    remote(qkv_ref.at[0, 1], kv.at[slot, part], kv_s.at[0, 0, 0], kv_r.at[slot, part], me, z).wait_recv()
+                    remote(k_ref.at[0], kv.at[slot, part], kv_s.at[0, 0, 0], kv_r.at[slot, part], me, z).wait_recv()
                     if relay and part == 0 and d == 2:
                         @pl.when(chip == 3)
                         def _():
@@ -311,6 +314,7 @@
     swap = remote(hout.at[1 - core], hother, h_sem.at[0], h_sem.at[1], sib, z)
     swap.start()
     w_copy.wait()
+    prt[...] = dot(hout[core], w[core])
     swap.wait()
 
     chunk = tok // nz
@@ -320,10 +324,10 @@
     def at(p):
         return pl.ds(pl.multiple_of(p * cols, cols), cols)
 
+    prt[...] += dot(hother[...], w[1 - core])
+
     def partial(d, p):
-        own = hout[core, d * chunk:(d + 1) * chunk, :]
-        other = hother[d * chunk:(d + 1) * chunk, :]
-        return dot(own, w[core, :, at(p)]) + dot(other, w[1 - core, :, at(p)])
+        return prt[d * chunk:(d + 1) * chunk, at(p)]
 
     def right(d, p):
         return remote(rsend.at[d, p], rrecv.at[d, p], rs_s.at[d, p], rs_r.at[d, p], me, (z + 1) % nz)
@@ -331,38 +335,49 @@
     def left(d, p):
         return remote(lsend.at[d, p], lrecv.at[d, p], ls_s.at[d, p], ls_r.at[d, p], me, (z + nz - 1) % nz)
 
-    for k in range(nz - 1):
-        d, e = nz - 1 - k, k
-
-        @pl.loop(0, pieces)
-        def _(p):
-            @pl.when(z < d)
-            def _():
+    def go_right(d):
+        @pl.when(z < d)
+        def _():
+            @pl.loop(0, pieces)
+            def _(p):
                 @pl.when(z == 0)
                 def _():
                     rsend[d, p] = partial(d, p).astype(BF16)
 
                 @pl.when(z > 0)
                 def _():
-                    mine = partial(d, p)
                     right(d, p).wait_recv()
-                    rsend[d, p] = (mine + rrecv[d, p].astype(F32)).astype(BF16)
+                    rsend[d, p] = (partial(d, p) + rrecv[d, p].astype(F32)).astype(BF16)
 
                 right(d, p).start()
 
-            @pl.when(z > e)
-            def _():
+    def go_left(d):
+        @pl.when(z > d)
+        def _():
+            @pl.loop(0, pieces)
+            def _(p):
                 @pl.when(z == nz - 1)
                 def _():
-                    lsend[e, p] = partial(e, p).astype(BF16)
+                    lsend[d, p] = partial(d, p).astype(BF16)
 
                 @pl.when(z < nz - 1)
                 def _():
-                    mine = partial(e, p)
-                    left(e, p).wait_recv()
-                    lsend[e, p] = (mine + lrecv[e, p].astype(F32)).astype(BF16)
-
-                left(e, p).start()
+                    left(d, p).wait_recv()
+                    lsend[d, p] = (partial(d, p) + lrecv[d, p].astype(F32)).astype(BF16)
+
+                left(d, p).start()
+
+    @pl.when(z < nz // 2)
+    def _():
+        for k in range(nz - 1):
+            go_right(nz - 1 - k)
+            go_left(k)
+
+    @pl.when(z >= nz // 2)
+    def _():
+        for k in range(nz - 1):
+            go_left(k)
+            go_right(nz - 1 - k)
 
     for d in range(nz):
         @pl.when(z == d)
@@ -407,22 +422,21 @@
     n, nz = lax.axis_size("seq"), lax.axis_size("head")
     half = heads // 2
     back = max(WINDOW // (2 * tok), 1)
-    qkv = jnp.stack((queries, keys, values)).reshape(3, tok, 2, half, width)
-    qkv = jnp.transpose(qkv, (2, 0, 3, 1, 4))
+    by_head = [jnp.transpose(x, (1, 0, 2)).reshape(2, half, tok, width) for x in (queries, keys, values)]
     fs = jnp.concatenate((log_forget.reshape(2, half, tok), strength.reshape(2, half, tok)), axis=1)
     model = out_weight.shape[1]
     weight = out_weight.reshape(2, half * width, model)
     chunk = tok // nz
     slots = 2 * back + 2
     chains = 2 * half
-    pieces = 4
+    pieces = 2
     far = max(n - 2 * (back + 1), 1)
     dma = pltpu.SemaphoreType.DMA
     vmem = pl.BlockSpec(memory_space=pltpu.VMEM)
     return pl.pallas_call(
         functools.partial(kernel, n, nz, back),
         out_shape=jax.ShapeDtypeStruct((chunk, model), BF16),
-        in_specs=[vmem, vmem, pl.BlockSpec(memory_space=pl.ANY)],
+        in_specs=[vmem, vmem, vmem, vmem, pl.BlockSpec(memory_space=pl.ANY)],
         out_specs=vmem,
         scratch_shapes=[
             pltpu.VMEM((slots, 2, half, tok, width), BF16),
@@ -442,18 +456,19 @@
             pltpu.VMEM((chains, tok, width), F32),
             pltpu.VMEM((2, tok, half * width), BF16),
             pltpu.VMEM((tok, half * width), BF16),
+            pltpu.VMEM((tok, model), F32),
             pltpu.VMEM((nz, pieces, chunk, model // pieces), BF16),
             pltpu.VMEM((nz, pieces, chunk, model // pieces), BF16),
             pltpu.VMEM((nz, pieces, chunk, model // pieces), BF16),
             pltpu.VMEM((nz, pieces, chunk, model // pieces), BF16),
             dma(()),
-            dma((back, 2, 2)), dma((slots, 2)), dma((2,)), dma(()), dma((n,)), dma((n,)),
+            dma((back, 2, 2)), dma((slots, 2)), dma((3,)), dma(()), dma((n,)), dma((n,)),
             dma((n,)), dma((n,)), dma((2,)), dma((2,)),
             dma((nz, pieces)), dma((nz, pieces)), dma((nz, pieces)), dma((nz, pieces)),
         ],
         compiler_params=pltpu.CompilerParams(
             collective_id=0, has_side_effects=True, vmem_limit_bytes=56 * 1024 * 1024),
-    )(qkv, fs, weight)
+    )(*by_head, fs, weight)
 
 
 def solution(mesh):

time: 84 us -> 67.5 us (0.80)
  Pallas kernels: 76.3 us -> 57.5 us
  local copies, waits for them, and re-layouts: 4.7 us -> 8.12 us
  other arithmetic: 1.57 us -> 0.6 us
    pallas_call x1, Pallas kernels: 76.3 us -> 57.5 us  [on_device(): pl.pallas_call(functools.partial(kernel, n, nz, back), out_shape=jax.Shap...]
    transpose x0 -> x3, local copies, waits for them, and re-layouts: none -> 5.05 us  [on_device(): jnp.transpose(x, (1, 0, 2)).reshape(2, half, tok, width)]
    unnamed x8 -> x1, local copies, waits for them, and re-layouts: 4.67 us -> 1.67 us
    transpose x1 -> x0, other arithmetic: 0.97 us -> none  [on_device(): qkv = jnp.transpose(qkv, (2, 0, 3, 1, 4))]
where the time goes in v3:
time: 67.5 us; the launch traced here: 66.2 us
  Pallas kernels  57.5 us (85%)
  local copies, waits for them, and re-layouts  8.12 us (12%)
    pallas_call x1, Pallas kernels, on_device(): pl.pallas_call(functools.partial(kernel, n, nz, back), out_shape=jax.Shap...  57.5 us
    transpose x3, local copies, waits for them, and re-layouts, on_device(): jnp.transpose(x, (1, 0, 2)).reshape(2, half, tok, width)  5.05 us
    unnamed x1, local copies, waits for them, and re-layouts  1.67 us

profile of v3, /device:TPU:4, one launch (start us, length us, event | category | flops | bytes accessed | tf_op | source)
XLA Modules:
  0.0 66.2 jit_solution(2952658139362031626)
XLA Ops:
  0.0 0.7 %reshape.21 = f32[2,2,256]{2,1,0:T(2,128)S(1)} reshape(f32[4,256]{1,0:T(4,128)} %param.9) | data formatting | bytes 8192 | tf_op jit(solution)/shard_map/reshape | solution.py:426
  0.7 0.7 %reshape.22 = f32[2,2,256]{2,1,0:T(2,128)S(1)} reshape(f32[4,256]{1,0:T(4,128)} %param.10) | data formatting | bytes 8192 | tf_op jit(solution)/shard_map/reshape | solution.py:426
  1.4 0.6 pad_maximum_fusion.fs_ref
  2.0 1.7 %copy.7 = bf16[4,256,128]{2,1,0:T(8,128)(2,1)} copy(bf16[4,256,128]{2,0,1:T(4,128)(2,1)} %bitcast.11) | data formatting | bytes 524288 | tf_op jit(solution)/shard_map/transpose | solution.py:425
  3.7 1.7 %copy.8 = bf16[4,256,128]{2,1,0:T(8,128)(2,1)} copy(bf16[4,256,128]{2,0,1:T(4,128)(2,1)} %bitcast.12) | data formatting | bytes 524288 | tf_op jit(solution)/shard_map/transpose | solution.py:425
  5.4 1.7 %copy.9 = bf16[4,256,128]{2,1,0:T(8,128)(2,1)} copy(bf16[4,256,128]{2,0,1:T(4,128)(2,1)} %bitcast.13) | data formatting | bytes 524288 | tf_op jit(solution)/shard_map/transpose | solution.py:425
  7.0 57.5 %shard_map.64 = bf16[64,2048]{1,0:T(8,128)(2,1)} custom-call(bf16[2,2,256,128]{3,2,1,0:T(8,128)(2,1)} %bitcast.8, bf16[2,2,256,128]{3,2,1,0:T(8,128)(2,1)} %bitcast.9, bf16[2,2,256,128]{3,2,1,0:T(8,128)(2,1)} %bitcast.10, f32[2,4,256]{2,1,0:T(4,128)} %pad_maximum_fusion.fs_ref, bf16[2,256,2048]{2,1,0:T(8,128)(2,1)} %bitcast.7), custom_call_target="tpu_custom_call" | custom-call | tf_op jit(solution)/shard_map/pallas_call | solution.py:436
  64.6 1.7 %copy.11 = bf16[64,2048]{1,0:T(8,128)(2,1)} copy(bf16[64,2048]{1,0:T(8,128)(2,1)} %shard_map.64) | data formatting | bytes 524288
